TPU v7x, 32 devices: a whole 2x2x4 slice. The times are simulated.
32 devices in a mesh: groups: 2 (over x), frames: 16 (over z, y, core).
Axes of the slice: x: 2, y: 2, z: 4, core: 2. Of those that a mesh axis runs over, the one named last changes fastest.
Arguments:
- video: float32 [4, 16, 256, 256], P('groups', 'frames'), parts along dimension 0, may hold values from -9 to 9
- clip_start: int32 [4], P('groups'), parts along dimension 0, may hold values from 0 to 7
- gain_space: float32 [256], replicated, may hold values from 0.1 to 1.9
- qkv_space: float32 [256, 768], replicated, may hold values from -0.375 to 0.375
- out_space: float32 [256, 256], replicated, may hold values from -0.375 to 0.375
- gain_time: float32 [256], replicated, may hold values from 0.1 to 1.9
- qkv_time: float32 [256, 768], replicated, may hold values from -0.375 to 0.375
- out_time: float32 [256, 256], replicated, may hold values from -0.375 to 0.375
- code_sums: float32 [8192, 256], P(('groups', 'frames')), parts along dimension 0, may hold values from -12 to 12
- code_counts: float32 [8192], P(('groups', 'frames')), parts along dimension 0, may hold values from 1 to 10
Outputs:
- latents: float32 [4, 16, 256, 256], P('groups', None, 'frames'), parts along dimension 0
- new_sums: float32 [8192, 256], P(('groups', 'frames')), parts along dimension 0
- new_counts: float32 [8192], P(('groups', 'frames')), parts along dimension 0
- new_codebook: float32 [8192, 256], P(('groups', 'frames')), parts along dimension 0
There are 2 independent parts, one for each index of `groups`. A program takes and returns all parts, laid end to end along the dimension named above; an argument that names none is the same for every part. Nothing has to cross between parts.
All inputs are finite; a program needn't handle non-finite values.
Results may differ from a plain program's by a relative error of at most 0.0003.
Values sent between devices are 32-bit elements; how exact they have to be, the bound alone decides.
A program may use at most 64 MiB of HBM per device.

v0:
```python
import jax
import jax.numpy as jnp
from jax import lax
from jax.sharding import PartitionSpec as P

HEADS = 4
ATTN_SCALE = 10.0
SOFTMAX_WARMTH = 0.05
DECAY_RATE = 0.9
EPSILON = 1e-06
TOP_PRECISION = lax.Precision.HIGHEST


def rms_norm(values, gain_vec):
    return values * lax.rsqrt(jnp.mean(values * values, -1, keepdims=True) + EPSILON) * gain_vec


def unit_vec(values):
    return values * lax.rsqrt(jnp.sum(values * values, -1, keepdims=True) + EPSILON)


def spatial_block(one_frame, gain_vec, w_qkv, w_out):
    width = one_frame.shape[-1]
    normed = rms_norm(one_frame, gain_vec)
    packed = jnp.dot(normed, w_qkv, precision=TOP_PRECISION)
    queries = unit_vec(packed[:, :width].reshape(-1, HEADS, width // HEADS))
    key_vecs = unit_vec(packed[:, width : 2 * width].reshape(-1, HEADS, width // HEADS))
    values = packed[:, 2 * width :].reshape(-1, HEADS, width // HEADS)
    scores = ATTN_SCALE * jnp.einsum("qhd,khd->hqk", queries, key_vecs, precision=TOP_PRECISION)
    assignment_weights = jnp.exp(scores)
    totals = jnp.sum(assignment_weights, -1).T[:, :, None]
    mixed = jnp.einsum("hqk,khd->qhd", assignment_weights, values, precision=TOP_PRECISION) / totals
    return one_frame + jnp.dot(mixed.reshape(-1, width), w_out, precision=TOP_PRECISION)


def time_block(spaced, clip_start, gain_vec, w_qkv, w_out):
    clips, frames, places, width = spaced.shape
    normed = rms_norm(spaced, gain_vec)
    packed = jnp.einsum("ctpd,de->ctpe", normed, w_qkv, precision=TOP_PRECISION)
    shape_heads = (clips, frames, places, HEADS, width // HEADS)
    queries = unit_vec(packed[..., :width].reshape(shape_heads))
    key_vecs = unit_vec(packed[..., width : 2 * width].reshape(shape_heads))
    values = packed[..., 2 * width :].reshape(shape_heads)
    scores = ATTN_SCALE * jnp.einsum(
        "ctphd,csphd->cphts", queries, key_vecs, precision=TOP_PRECISION
    )
    later = jnp.arange(frames, dtype=jnp.int32)[:, None]
    earlier = jnp.arange(frames, dtype=jnp.int32)[None, :]
    allowed = (earlier <= later)[None] & (
        (earlier[None] >= clip_start[:, None, None]) | (earlier == later)[None]
    )
    assignment_weights = jnp.exp(scores) * allowed[:, None, None, :, :].astype(jnp.float32)
    totals = jnp.transpose(jnp.sum(assignment_weights, -1), (0, 3, 1, 2))[..., None]
    mixed = (
        jnp.einsum("cphts,csphd->ctphd", assignment_weights, values, precision=TOP_PRECISION)
        / totals
    )
    return spaced + jnp.einsum(
        "ctpd,de->ctpe", mixed.reshape(clips, frames, places, width), w_out, precision=TOP_PRECISION
    )


def local(
    video,
    clip_start,
    gain_space,
    qkv_space,
    out_space,
    gain_time,
    qkv_time,
    out_time,
    code_sums,
    code_counts,
):
    clips, local_frames, places, width = video.shape
    flat_frames = video.reshape(clips * local_frames, places, width)
    spaced = lax.map(
        lambda one_frame: spatial_block(one_frame, gain_space, qkv_space, out_space), flat_frames
    )
    spaced = spaced.reshape(clips, local_frames, places, width)
    by_place = lax.all_to_all(spaced, "frames", split_axis=2, concat_axis=1, tiled=True)
    latents = time_block(by_place, clip_start, gain_time, qkv_time, out_time)
    unit_token_vectors = unit_vec(latents.reshape(-1, width))
    local_codes = unit_vec(code_sums / code_counts[:, None])
    codebook_matrix = lax.all_gather(local_codes, "frames", axis=0, tiled=True)
    assignment_weights = jnp.exp(
        jnp.dot(unit_token_vectors, codebook_matrix.T, precision=TOP_PRECISION) / SOFTMAX_WARMTH
    )
    probs = assignment_weights / jnp.sum(assignment_weights, 1, keepdims=True)
    term_sums = lax.dot_general(
        probs, unit_token_vectors, (((0,), (0,)), ((), ())), precision=TOP_PRECISION
    )
    term_counts = jnp.sum(probs, 0)
    got_sums, got_counts = (
        lax.psum_scatter(term_sums, "frames", scatter_dimension=0, tiled=True),
        lax.psum_scatter(term_counts, "frames", scatter_dimension=0, tiled=True),
    )
    new_sums = DECAY_RATE * code_sums + (1.0 - DECAY_RATE) * got_sums
    new_counts = DECAY_RATE * code_counts + (1.0 - DECAY_RATE) * got_counts
    new_codebook = new_sums / new_counts[:, None]
    return (latents, new_sums, new_counts, new_codebook)


def solution(mesh):
    in_specs = (
        P("groups", "frames", None, None),
        P("groups"),
        P(),
        P(),
        P(),
        P(),
        P(),
        P(),
        P(("groups", "frames"), None),
        P(("groups", "frames")),
    )
    out_specs = (
        P("groups", None, "frames", None),
        P(("groups", "frames"), None),
        P(("groups", "frames")),
        P(("groups", "frames"), None),
    )
    return jax.shard_map(local, mesh=mesh, in_specs=in_specs, out_specs=out_specs, check_vma=False)
```

profile of v0, /device:TPU:0, one launch (start us, length us, event | category | flops | bytes accessed | tf_op | source)
XLA Modules:
  0.0 198.9 jit_solution(9034979632726046601)
XLA Ops:
  7.2 1.2 multiply_reduce_fusion.6
  8.4 1.8 broadcast_multiply_fusion.2
  10.3 25.9 %while.10 = (s32[]{:T(128)}, f32[2,256,256]{2,0,1:T(2,128)}, f32[2,256,256]{2,1,0:T(8,128)}, f32[256]{0:T(256)}, f32[256,768]{1,0:T(8,128)}, /*index=5*/f32[256,256]{1,0:T(8,128)}, s32[]{:T(128)}, s32[]{:T(128)}) while((s32[]{:T(128)}, f32[2,256,256]{2,0,1:T(2,128)}, f32[2,256,256]{2,1,0:T(8,128)}, f32[256]{0:T(256)}, f32[256,768]{1,0:T(8,128)}, ...), condition=%wide.region_5.6_spmd, body=%wide.region_0.5_spmd.sunk | while | flops 1209269504 | bytes 14202521 | solution.py:77
  10.3 1.1 fusion.67
  11.5 2.1 %fusion.68 = f32[256,768]{1,0:T(8,128)S(1)} fusion(f32[256,768]{1,0:T(8,128)} %get-tuple-element.142, f32[2,256,256]{2,1,0:T(8,128)} %get-tuple-element.140, s32[]{:T(128)} %get-tuple-element.130, f32[256]{0:T(256)} %get-tuple-element.141, f32[256]{0:T(256)S(1)} %add_rsqrt_fusion.10), kind=kOutput, calls=%fused_computation.10.clone.1 | convolution fusion | flops 604110848 | bytes 1837568 | tf_op jit(solution)/shard_map/while/body/eval_jaxpr/dot_general | solution.py:25
  14.0 1.1 fusion.70
  15.3 0.8 fusion.71
  16.9 6.3 %dynamic_update_slice.5 = f32[2,256,256]{2,0,1:T(2,128)} dynamic-update-slice(f32[2,256,256]{2,0,1:T(2,128)} %get-tuple-element.131, f32[1,256,256]{2,0,1:T(1,128)S(1)} %copy.85, s32[]{:T(128)} %get-tuple-element.130, s32[]{:T(128)} %constant.22.clone.1..sunk, s32[]{:T(128)} %constant.22.clone.1..sunk) | dynamic-update-slice | bytes 524292 | tf_op jit(solution)/shard_map/while/body/jit(dynamic_update_index_in_dim)/dynamic_update_slice | solution.py:77
  23.3 1.1 fusion.67
  24.4 2.1 %fusion.68 = f32[256,768]{1,0:T(8,128)S(1)} fusion(f32[256,768]{1,0:T(8,128)} %get-tuple-element.142, f32[2,256,256]{2,1,0:T(8,128)} %get-tuple-element.140, s32[]{:T(128)} %get-tuple-element.130, f32[256]{0:T(256)} %get-tuple-element.141, f32[256]{0:T(256)S(1)} %add_rsqrt_fusion.10), kind=kOutput, calls=%fused_computation.10.clone.1 | convolution fusion | flops 604110848 | bytes 1837568 | tf_op jit(solution)/shard_map/while/body/eval_jaxpr/dot_general | solution.py:25
  26.9 1.1 fusion.70
  28.2 0.8 fusion.71
  29.9 6.3 %dynamic_update_slice.5 = f32[2,256,256]{2,0,1:T(2,128)} dynamic-update-slice(f32[2,256,256]{2,0,1:T(2,128)} %get-tuple-element.131, f32[1,256,256]{2,0,1:T(1,128)S(1)} %copy.85, s32[]{:T(128)} %get-tuple-element.130, s32[]{:T(128)} %constant.22.clone.1..sunk, s32[]{:T(128)} %constant.22.clone.1..sunk) | dynamic-update-slice | bytes 524292 | tf_op jit(solution)/shard_map/while/body/jit(dynamic_update_index_in_dim)/dynamic_update_slice | solution.py:77
  36.2 7.4 %all-to-all-start = ((f32[2,1,256,256]{3,0,1,2:T(2,128)}), f32[2,1,256,256]{3,0,1,2:T(2,128)S(1)}, u32[]{:S(2)}, u32[]{:S(2)}) async-start(f32[2,1,256,256]{3,0,1,2:T(2,128)} %bitcast.103), calls=%async_computation | async-start | bytes 1048576 | tf_op jit(solution)/shard_map/all_to_all | solution.py:81
  43.8 22.8 %all-to-all-done = f32[2,1,256,256]{3,0,1,2:T(2,128)S(1)} async-done(((f32[2,1,256,256]{3,0,1,2:T(2,128)}), f32[2,1,256,256]{3,0,1,2:T(2,128)S(1)}, u32[]{:S(2)}, u32[]{:S(2)}) %all-to-all-start) | async-done | bytes 524320 | tf_op jit(solution)/shard_map/all_to_all | solution.py:81
  67.3 1.5 fusion.23
  68.8 1.2 fusion.37
  70.4 1.5 reshape.171
  71.9 2.5 %reshape.170 = f32[2,16,16,4,64]{4,3,2,1,0:T(4,128)} reshape(f32[2,16,16,256]{3,2,1,0:T(8,128)} %get-tuple-element.58) | data formatting | bytes 1048576 | tf_op jit(solution)/shard_map/reshape | solution.py:43
  74.9 0.6 multiply_reduce_fusion.3
  75.7 1.5 broadcast_multiply_fusion
  77.1 3.1 %fusion.38 = (f32[2,16,4,16]{3,2,1,0:T(4,128)S(1)}, f32[2,16,4,16,16]{3,4,2,1,0:T(8,128)S(1)}) fusion(f32[2,16,16]{1,2,0:T(8,128)S(1)} %and_convert_fusion, f32[2,16,16,4,64]{4,3,2,1,0:T(4,128)S(1)} %get-tuple-element.69, f32[2,16,16,4,64]{4,3,2,1,0:T(4,128)S(1)} %get-tuple-element.70), kind=kOutput, calls=%fused_computation.72 | convolution fusion | flops 25262080 | bytes 1189888 | tf_op jit(solution)/shard_map/ctphd,csphd->cphts/dot_general | solution.py:44
  80.3 2.5 %fusion.17 = f32[2,16,16,4,64]{4,1,3,2,0:T(8,128)S(1)} fusion(f32[2,16,4,16,16]{3,4,2,1,0:T(8,128)S(1)} %get-tuple-element.62, f32[2,16,16,4,64]{4,3,2,1,0:T(4,128)S(1)} %copy-done.6, f32[2,16,16,4]{1,3,2,0:T(4,128)S(1)} %bitcast.106), kind=kOutput, calls=%fused_computation.28 | convolution fusion | flops 25296896 | bytes 1187840 | tf_op jit(solution)/shard_map/cphts,csphd->ctphd/dot_general | solution.py:55
  83.3 0.6 reshape.173
  83.9 1.6 multiply_reduce_fusion.4
  85.8 9.9 %fusion.16 = (f32[512]{0:T(512)S(1)}, f32[512,4096]{1,0:T(8,128)S(1)}) fusion(f32[512,256]{1,0:T(8,128)S(1)} %bitcast_multiply_fusion.2, f32[4096,256]{1,0:T(8,128)} %all-gather.2.cloned.1.call-done), kind=kOutput, calls=%fused_computation.26 | convolution fusion | flops 6446644736 | bytes 13109248 | tf_op jit(solution)/shard_map/dot_general | solution.py:87
  95.7 3.2 %copy-done.1 = f32[512,4096]{1,0:T(8,128)} copy-done((f32[512,4096]{1,0:T(8,128)}, f32[512,4096]{1,0:T(8,128)S(1)}, u32[]{:S(2)}) %copy-start.1) | copy-done | bytes 8388632
  98.9 15.0 %fusion.28 = f32[4096,256]{1,0:T(8,128)} fusion(f32[512,256]{1,0:T(8,128)S(1)} %bitcast_multiply_fusion.2, f32[512,4096]{1,0:T(8,128)S(1)} %get-tuple-element.66, f32[512]{0:T(512)S(1)} %get-tuple-element.65), kind=kOutput, calls=%fused_computation.48 | convolution fusion | flops 6446645248 | bytes 13109248 | tf_op jit(solution)/shard_map/dot_general | solution.py:90
  115.2 4.3 %fusion.27 = f32[4096]{0:T(1024)S(1)} fusion(f32[512]{0:T(512)S(1)} %get-tuple-element.65, f32[512,4096]{1,0:T(8,128)} %copy-done.1), kind=kLoop, calls=%fused_computation.47 | loop fusion | flops 6287360 | bytes 8407040 | tf_op jit(solution)/shard_map/reduce_sum | solution.py:93
  119.5 64.5 %all-reduce = f32[4096]{0:T(1024)S(1)} all-reduce(f32[4096]{0:T(1024)S(1)} %fusion.27), channel_id=3, replica_groups=mesh['groups'=2,'frames'=16] {'frames'}, use_global_device_ids=true, to_apply=%region_15.16.clone | all-reduce | flops 4096 | bytes 32768
  184.1 6.2 %reduce-scatter.2.cloned.1.call-done = f32[256,256]{1,0:T(8,128)} async-done(((f32[4096,256]{1,0:T(8,128)}), f32[256,256]{1,0:T(8,128)}) %reduce-scatter.2.cloned.1.call-update) | async-done | bytes 262160 | tf_op jit(solution)/shard_map/reduce_scatter | solution.py:95
  190.3 1.8 broadcast_divide_fusion
  (71 shorter events, 6.2 us)
Async XLA Ops:
  7.2 60.1 %copy-start = (f32[256,768]{1,0:T(8,128)S(1)}, f32[256,768]{1,0:T(8,128)}, u32[]{:S(2)}) copy-start(f32[256,768]{1,0:T(8,128)} %param.18) | copy-start | bytes 2359300
  7.2 78.6 %all-gather.2.cloned.1.call-start = ((), (), s32[]{:S(2)}) async-start(), calls=%async_computation.2 | async-start | bytes 4456448 | tf_op jit(solution)/shard_map/all_gather | solution.py:85
  10.3 33.4 %copy-start.10 = (s32[2]{0:T(128)S(1)}, s32[2]{0:T(128)}, u32[]{:S(2)}) copy-start(s32[2]{0:T(128)} %param.13) | copy-start | bytes 28
  10.3 57.0 %copy-start.9 = (f32[256]{0:T(256)S(1)}, f32[256]{0:T(256)}, u32[]{:S(2)}) copy-start(f32[256]{0:T(256)} %param.17) | copy-start | bytes 3076
  10.3 5.7 %copy-start.2 = (f32[2,256,256]{2,1,0:T(8,128)S(1)}, f32[2,256,256]{2,1,0:T(8,128)}, u32[]{:S(2)}) copy-start(f32[2,256,256]{2,1,0:T(8,128)} %get-tuple-element.140) | copy-start | bytes 1572868 | tf_op jit(solution)/shard_map/while
  10.3 5.7 %copy-start.3 = (f32[256,256]{1,0:T(8,128)S(1)}, f32[256,256]{1,0:T(8,128)}, u32[]{:S(2)}) copy-start(f32[256,256]{1,0:T(8,128)} %get-tuple-element.143) | copy-start | bytes 786436 | tf_op jit(solution)/shard_map/while
  23.3 5.7 %copy-start.2 = (f32[2,256,256]{2,1,0:T(8,128)S(1)}, f32[2,256,256]{2,1,0:T(8,128)}, u32[]{:S(2)}) copy-start(f32[2,256,256]{2,1,0:T(8,128)} %get-tuple-element.140) | copy-start | bytes 1572868 | tf_op jit(solution)/shard_map/while
  23.3 5.7 %copy-start.3 = (f32[256,256]{1,0:T(8,128)S(1)}, f32[256,256]{1,0:T(8,128)}, u32[]{:S(2)}) copy-start(f32[256,256]{1,0:T(8,128)} %get-tuple-element.143) | copy-start | bytes 786436 | tf_op jit(solution)/shard_map/while
  36.2 30.5 %all-to-all-start = ((f32[2,1,256,256]{3,0,1,2:T(2,128)}), f32[2,1,256,256]{3,0,1,2:T(2,128)S(1)}, u32[]{:S(2)}, u32[]{:S(2)}) async-start(f32[2,1,256,256]{3,0,1,2:T(2,128)} %bitcast.103), calls=%async_computation | async-start | bytes 1048576 | tf_op jit(solution)/shard_map/all_to_all | solution.py:81
  43.6 146.7 %reduce-scatter.2.cloned.1.call-start = ((), (), s32[]{:S(2)}) async-start(), calls=%async_computation.3 | async-start | bytes 4456448 | tf_op jit(solution)/shard_map/reduce_scatter | solution.py:95
  74.3 6.0 %copy-start.6 = (f32[2,16,16,4,64]{4,3,2,1,0:T(4,128)S(1)}, f32[2,16,16,4,64]{4,3,2,1,0:T(4,128)}, u32[]{:S(2)}) copy-start(f32[2,16,16,4,64]{4,3,2,1,0:T(4,128)} %reshape.170) | copy-start | bytes 1572868
  85.5 28.5 %copy-start.5 = (f32[2,16,16,256]{3,2,1,0:T(8,128)}, f32[2,16,16,256]{3,2,1,0:T(8,128)S(1)}, u32[]{:S(2)}) copy-start(f32[2,16,16,256]{3,2,1,0:T(8,128)S(1)} %get-tuple-element.64) | copy-start | bytes 1572868
  95.7 3.2 %copy-start.1 = (f32[512,4096]{1,0:T(8,128)}, f32[512,4096]{1,0:T(8,128)S(1)}, u32[]{:S(2)}) copy-start(f32[512,4096]{1,0:T(8,128)S(1)} %get-tuple-element.66) | copy-start | bytes 25165828
  98.9 15.1 %copy-start.11 = (u32[32]{0:T(128)S(1)}, u32[32]{0:T(128)}, u32[]{:S(2)}) copy-start(u32[32]{0:T(128)} %constant.46) | copy-start | bytes 388
  114.0 70.1 %copy-start.7 = (f32[256]{0:T(256)S(1)}, f32[256]{0:T(256)}, u32[]{:S(2)}) copy-start(f32[256]{0:T(256)} %param.21) | copy-start | bytes 3076
  114.0 76.3 %copy-start.4 = (f32[256,256]{1,0:T(8,128)S(1)}, f32[256,256]{1,0:T(8,128)}, u32[]{:S(2)}) copy-start(f32[256,256]{1,0:T(8,128)} %param.20) | copy-start | bytes 786436
  184.1 8.0 %copy-start.8 = (f32[256]{0:T(256)}, f32[256]{0:T(256)S(1)}, u32[]{:S(2)}) copy-start(f32[256]{0:T(256)S(1)} %fusion.33) | copy-start | bytes 3076
Sparse Core Ops, SparseCore 0:
  10.7 62.2 all-gather.1
  114.1 76.1 reduce-scatter.1
where the time goes:
time: 200 us; the launch traced here: 199 us
  blocking collectives  64.5 us (32%)
  matrix products  42.9 us (21%)
  waiting for transfers between devices  29.1 us (15%)
  local copies, waits for them, and re-layouts  24.8 us (12%)
  other arithmetic  15 us (8%)
  between operations  14.9 us (7%)
  starting transfers between devices  7.5 us (4%)
    unnamed x1, blocking collectives  64.5 us
    all_to_all x1, waiting for transfers between devices, local(): lax.all_to_all(spaced, 'frames', split_axis=2, concat_axis=1, tiled=True)  22.8 us
    dot_general x1, matrix products, local(): lax.dot_general(probs, unit_token_vectors, (((0,), (0,)), ((), ())), prec...  15 us
    dynamic_update_slice x4, local copies, waits for them, and re-layouts, local(): lax.map(lambda one_frame: spatial_block(one_frame, gain_space, qkv_space,...  13.2 us
    dot_general x1, matrix products, local(): jnp.dot(unit_token_vectors, codebook_matrix.T, precision=TOP_PRECISION)  9.91 us
    all_to_all x1, starting transfers between devices, local(): lax.all_to_all(spaced, 'frames', split_axis=2, concat_axis=1, tiled=True)  7.42 us
    reduce_scatter x1, waiting for transfers between devices, local(): lax.psum_scatter(term_sums, 'frames', scatter_dimension=0, tiled=True)  6.17 us
    reduce_sum x1, other arithmetic, local(): term_counts = jnp.sum(probs, 0)  4.27 us
  transfers between devices with their start and end apart: 3, of which 2 were waited for; matrix products, arithmetic and copies ran while one was open for 25% of the time, Pallas kernels for 0%

commit v1 on v0

--- a/solution.py
+++ b/solution.py
@@ -9,6 +9,28 @@
 DECAY_RATE = 0.9
 EPSILON = 1e-06
 TOP_PRECISION = lax.Precision.HIGHEST
+
+
+def split_up(value, dim, count):
+    before, after = (value.shape[:dim], value.shape[dim + 1 :])
+    return jnp.moveaxis(value.reshape(*before, count, -1, *after), dim, 0)
+
+
+def joined_along(parts, dim):
+    dims = list(parts.shape[1:])
+    dims[dim] *= parts.shape[0]
+    return jnp.moveaxis(parts, 0, dim).reshape(dims)
+
+
+def pairwise_exchange(array, axis, split_dim, concat_dim):
+    peers, mine = (lax.axis_size(axis), lax.axis_index(axis))
+    blocks = split_up(array, split_dim, peers)
+    outs = [blocks[mine]]
+    for step in range(1, peers):
+        sent = blocks[mine ^ step]
+        outs.append(lax.ppermute(sent, axis, [(i, i ^ step) for i in range(peers)]))
+    blocks = jnp.stack(outs)[mine ^ jnp.arange(peers)]
+    return joined_along(blocks, concat_dim)
 
 
 def rms_norm(values, gain_vec):
@@ -78,7 +100,7 @@
         lambda one_frame: spatial_block(one_frame, gain_space, qkv_space, out_space), flat_frames
     )
     spaced = spaced.reshape(clips, local_frames, places, width)
-    by_place = lax.all_to_all(spaced, "frames", split_axis=2, concat_axis=1, tiled=True)
+    by_place = pairwise_exchange(spaced, "frames", 2, 1)
     latents = time_block(by_place, clip_start, gain_time, qkv_time, out_time)
     unit_token_vectors = unit_vec(latents.reshape(-1, width))
     local_codes = unit_vec(code_sums / code_counts[:, None])

time: 200 us -> 190 us (0.950)
  starting transfers between devices: 7.5 us -> 23.6 us
  waiting for transfers between devices: 29.1 us -> 18.2 us
  local copies, waits for them, and re-layouts: 24.8 us -> 13.9 us
  blocking collectives: 64.5 us -> 59.9 us
    ppermute x0 -> x15, starting transfers between devices: none -> 23.5 us  [pairwise_exchange(): outs.append(lax.ppermute(sent, axis, [(i, i ^ step) for i in range(peers)]))]
    all_to_all x1 -> x0, waiting for transfers between devices: 22.8 us -> none  [local(): lax.all_to_all(spaced, 'frames', split_axis=2, concat_axis=1, tiled=True)]
    dynamic_update_slice x4 -> x0, local copies, waits for them, and re-layouts: 13.2 us -> none  [local(): lax.map(lambda one_frame: spatial_block(one_frame, gain_space, qkv_space,...]
    all_to_all x1 -> x0, starting transfers between devices: 7.42 us -> none  [local(): lax.all_to_all(spaced, 'frames', split_axis=2, concat_axis=1, tiled=True)]
    reduce_scatter x1, waiting for transfers between devices: 6.17 us -> 12.4 us  [local(): lax.psum_scatter(term_sums, 'frames', scatter_dimension=0, tiled=True)]
    ppermute x0 -> x15, waiting for transfers between devices: none -> 5.78 us  [pairwise_exchange(): outs.append(lax.ppermute(sent, axis, [(i, i ^ step) for i in range(peers)]))]
    unnamed x1, blocking collectives: 64.5 us -> 59.9 us
    unnamed x21 -> x36, local copies, waits for them, and re-layouts: 3.85 us -> 4.67 us
  transfers between devices with their start and end apart: 3 -> 17, of which waited for: 2 -> 4; matrix products, arithmetic and copies ran while one was open for 25% -> 21% of each run, Pallas kernels for 0% -> 0%
where the time goes in v1:
time: 190 us
  blocking collectives  59.9 us (32%)
  matrix products  44.1 us (23%)
  starting transfers between devices  23.6 us (12%)
  waiting for transfers between devices  18.2 us (10%)
  between operations  15.1 us (8%)
  other arithmetic  14.8 us (8%)
  local copies, waits for them, and re-layouts  13.9 us (7%)
    unnamed x1, blocking collectives  59.9 us
    ppermute x15, starting transfers between devices, pairwise_exchange(): outs.append(lax.ppermute(sent, axis, [(i, i ^ step) for i in range(peers)]))  23.5 us
    dot_general x1, matrix products, local(): lax.dot_general(probs, unit_token_vectors, (((0,), (0,)), ((), ())), prec...  15.1 us
    reduce_scatter x1, waiting for transfers between devices, local(): lax.psum_scatter(term_sums, 'frames', scatter_dimension=0, tiled=True)  12.4 us
    dot_general x1, matrix products, local(): jnp.dot(unit_token_vectors, codebook_matrix.T, precision=TOP_PRECISION)  9.7 us
    ppermute x15, waiting for transfers between devices, pairwise_exchange(): outs.append(lax.ppermute(sent, axis, [(i, i ^ step) for i in range(peers)]))  5.78 us
    unnamed x36, local copies, waits for them, and re-layouts  4.67 us
    reduce_sum x1, other arithmetic, local(): term_counts = jnp.sum(probs, 0)  4.27 us
  transfers between devices with their start and end apart: 17, of which 4 were waited for; matrix products, arithmetic and copies ran while one was open for 21% of the time, Pallas kernels for 0%

profile of v1, /device:TPU:0, one launch (start us, length us, event | category | flops | bytes accessed | tf_op | source)
XLA Modules:
  0.0 189.7 jit_solution(9925320503380913837)
XLA Ops:
  7.2 1.2 multiply_reduce_fusion.5
  8.4 1.8 broadcast_multiply_fusion.2
  10.4 14.1 %while.10 = (s32[]{:T(128)}, f32[2,256,256]{2,1,0:T(8,128)}, f32[2,256,256]{2,1,0:T(8,128)}, f32[256]{0:T(256)}, f32[256,768]{1,0:T(8,128)}, /*index=5*/f32[256,256]{1,0:T(8,128)}, s32[]{:T(128)}) while((s32[]{:T(128)}, f32[2,256,256]{2,1,0:T(8,128)}, f32[2,256,256]{2,1,0:T(8,128)}, f32[256]{0:T(256)}, f32[256,768]{1,0:T(8,128)}, ...), condition=%wide.region_5.6_spmd, body=%wide.region_0.5_spmd.sunk | while | flops 1209269504 | bytes 13154441 | solution.py:99
  11.6 2.1 %fusion.72 = f32[256,768]{1,0:T(8,128)S(1)} fusion(f32[256,768]{1,0:T(8,128)} %get-tuple-element.155, f32[2,256,256]{2,1,0:T(8,128)} %get-tuple-element.153, s32[]{:T(128)} %get-tuple-element.144, f32[256]{0:T(256)} %get-tuple-element.154, f32[256]{0:T(256)S(1)} %add_rsqrt_fusion.10), kind=kOutput, calls=%fused_computation.12.clone.1 | convolution fusion | flops 604110848 | bytes 1837568 | tf_op jit(solution)/shard_map/while/body/eval_jaxpr/dot_general | solution.py:47
  16.2 1.3 fusion.76
  18.6 2.1 %fusion.72 = f32[256,768]{1,0:T(8,128)S(1)} fusion(f32[256,768]{1,0:T(8,128)} %get-tuple-element.155, f32[2,256,256]{2,1,0:T(8,128)} %get-tuple-element.153, s32[]{:T(128)} %get-tuple-element.144, f32[256]{0:T(256)} %get-tuple-element.154, f32[256]{0:T(256)S(1)} %add_rsqrt_fusion.10), kind=kOutput, calls=%fused_computation.12.clone.1 | convolution fusion | flops 604110848 | bytes 1837568 | tf_op jit(solution)/shard_map/while/body/eval_jaxpr/dot_general | solution.py:47
  23.2 1.3 fusion.76
  26.1 2.6 %collective-permute-start.1 = (f32[2,1,16,256]{3,2,0,1:T(8,128)S(1)}, f32[2,1,16,256]{3,2,0,1:T(8,128)S(1)}, u32[]{:S(2)}, u32[]{:S(2)}) collective-permute-start(f32[2,1,16,256]{3,2,0,1:T(8,128)S(1)} %get-tuple-element.74), channel_id=1, source_target_pairs={{0,2},{1,3},{2,0},{3,1},{4,6},{5,7},{6,4},{7,5},{8,10},{9,11},{10,... | collective-permute-start | bytes 98312 | tf_op jit(solution)/shard_map/ppermute | solution.py:31
  28.8 1.8 collective-permute-start.3
  31.5 2.7 %collective-permute-start.5 = (f32[2,1,16,256]{3,2,0,1:T(8,128)S(1)}, f32[2,1,16,256]{3,2,0,1:T(8,128)S(1)}, u32[]{:S(2)}, u32[]{:S(2)}) collective-permute-start(f32[2,1,16,256]{3,2,0,1:T(8,128)S(1)} %get-tuple-element.70), channel_id=1, source_target_pairs={{0,6},{1,7},{2,4},{3,5},{4,2},{5,3},{6,0},{7,1},{8,14},{9,15},{10,... | collective-permute-start | bytes 98312 | tf_op jit(solution)/shard_map/ppermute | solution.py:31
  34.4 2.7 %collective-permute-start.7 = (f32[2,1,16,256]{3,2,0,1:T(8,128)S(1)}, f32[2,1,16,256]{3,2,0,1:T(8,128)S(1)}, u32[]{:S(2)}, u32[]{:S(2)}) collective-permute-start(f32[2,1,16,256]{3,2,0,1:T(8,128)S(1)} %get-tuple-element.68), channel_id=1, source_target_pairs={{0,8},{1,9},{2,10},{3,11},{4,12},{5,13},{6,14},{7,15},{8,0},{9,1},... | collective-permute-start | bytes 98312 | tf_op jit(solution)/shard_map/ppermute | solution.py:31
  37.1 3.5 %collective-permute-start.9 = (f32[2,1,16,256]{3,2,0,1:T(8,128)S(1)}, f32[2,1,16,256]{3,2,0,1:T(8,128)S(1)}, u32[]{:S(2)}, u32[]{:S(2)}) collective-permute-start(f32[2,1,16,256]{3,2,0,1:T(8,128)S(1)} %get-tuple-element.66), channel_id=1, source_target_pairs={{0,10},{1,11},{2,8},{3,9},{4,14},{5,15},{6,12},{7,13},{8,2},{9,3},... | collective-permute-start | bytes 98312 | tf_op jit(solution)/shard_map/ppermute | solution.py:31
  40.7 3.5 %collective-permute-start.11 = (f32[2,1,16,256]{3,2,0,1:T(8,128)S(1)}, f32[2,1,16,256]{3,2,0,1:T(8,128)S(1)}, u32[]{:S(2)}, u32[]{:S(2)}) collective-permute-start(f32[2,1,16,256]{3,2,0,1:T(8,128)S(1)} %get-tuple-element.64), channel_id=1, source_target_pairs={{0,12},{1,13},{2,14},{3,15},{4,8},{5,9},{6,10},{7,11},{8,4},{9,5},... | collective-permute-start | bytes 98312 | tf_op jit(solution)/shard_map/ppermute | solution.py:31
  44.3 4.4 %collective-permute-start.13 = (f32[2,1,16,256]{3,2,0,1:T(8,128)S(1)}, f32[2,1,16,256]{3,2,0,1:T(8,128)S(1)}, u32[]{:S(2)}, u32[]{:S(2)}) collective-permute-start(f32[2,1,16,256]{3,2,0,1:T(8,128)S(1)} %get-tuple-element.62), channel_id=1, source_target_pairs={{0,14},{1,15},{2,12},{3,13},{4,10},{5,11},{6,8},{7,9},{8,6},{9,7},... | collective-permute-start | bytes 98312 | tf_op jit(solution)/shard_map/ppermute | solution.py:31
  48.7 1.4 collective-permute-start.14
  50.5 2.5 %collective-permute-done.13 = f32[2,1,16,256]{3,2,0,1:T(8,128)S(1)} collective-permute-done((f32[2,1,16,256]{3,2,0,1:T(8,128)S(1)}, f32[2,1,16,256]{3,2,0,1:T(8,128)S(1)}, u32[]{:S(2)}, u32[]{:S(2)}) %collective-permute-start.13) | collective-permute-done | bytes 32800 | tf_op jit(solution)/shard_map/ppermute | solution.py:31
  53.0 2.9 %collective-permute-done.14 = f32[2,1,16,256]{3,2,0,1:T(8,128)S(1)} collective-permute-done((f32[2,1,16,256]{3,2,0,1:T(8,128)S(1)}, f32[2,1,16,256]{3,2,0,1:T(8,128)S(1)}, u32[]{:S(2)}, u32[]{:S(2)}) %collective-permute-start.14) | collective-permute-done | bytes 32800 | tf_op jit(solution)/shard_map/ppermute | solution.py:31
  56.7 1.5 fusion.24
  58.1 1.2 fusion.41
  59.8 1.5 reshape.206
  61.3 2.5 %reshape.205 = f32[2,16,16,4,64]{4,3,2,1,0:T(4,128)} reshape(f32[2,16,16,256]{3,2,1,0:T(8,128)} %get-tuple-element.58) | data formatting | bytes 1048576 | tf_op jit(solution)/shard_map/reshape | solution.py:65
  65.1 1.5 broadcast_multiply_fusion
  66.5 3.1 %fusion.42 = (f32[2,16,4,16]{3,2,1,0:T(4,128)S(1)}, f32[2,16,4,16,16]{3,4,2,1,0:T(8,128)S(1)}) fusion(f32[2,16,16]{1,2,0:T(8,128)S(1)} %and_convert_fusion, f32[2,16,16,4,64]{4,3,2,1,0:T(4,128)S(1)} %get-tuple-element.84, f32[2,16,16,4,64]{4,3,2,1,0:T(4,128)S(1)} %get-tuple-element.85), kind=kOutput, calls=%fused_computation.110 | convolution fusion | flops 25262080 | bytes 1189888 | tf_op jit(solution)/shard_map/ctphd,csphd->cphts/dot_general | solution.py:66
  69.7 2.5 %fusion.18 = f32[2,16,16,4,64]{4,1,3,2,0:T(8,128)S(1)} fusion(f32[2,16,4,16,16]{3,4,2,1,0:T(8,128)S(1)} %get-tuple-element.77, f32[2,16,16,4,64]{4,3,2,1,0:T(4,128)S(1)} %copy-done.6, f32[2,16,16,4]{1,3,2,0:T(4,128)S(1)} %bitcast.215), kind=kOutput, calls=%fused_computation.30 | convolution fusion | flops 25296896 | bytes 1187840 | tf_op jit(solution)/shard_map/cphts,csphd->ctphd/dot_general | solution.py:77
  73.3 1.6 multiply_reduce_fusion.4
  75.2 9.7 %fusion.17 = (f32[512]{0:T(512)S(1)}, f32[512,4096]{1,0:T(8,128)S(1)}) fusion(f32[512,256]{1,0:T(8,128)S(1)} %bitcast_multiply_fusion.2, f32[4096,256]{1,0:T(8,128)} %all-gather.2.cloned.1.call-done), kind=kOutput, calls=%fused_computation.28 | convolution fusion | flops 6446644736 | bytes 13109248 | tf_op jit(solution)/shard_map/dot_general | solution.py:109
  84.9 3.2 %copy-done.1 = f32[512,4096]{1,0:T(8,128)} copy-done((f32[512,4096]{1,0:T(8,128)}, f32[512,4096]{1,0:T(8,128)S(1)}, u32[]{:S(2)}) %copy-start.1) | copy-done | bytes 8388632
  88.1 15.1 %fusion.31 = f32[4096,256]{1,0:T(8,128)} fusion(f32[512,256]{1,0:T(8,128)S(1)} %bitcast_multiply_fusion.2, f32[512,4096]{1,0:T(8,128)S(1)} %get-tuple-element.81, f32[512]{0:T(512)S(1)} %get-tuple-element.80), kind=kOutput, calls=%fused_computation.52 | convolution fusion | flops 6446645248 | bytes 13109248 | tf_op jit(solution)/shard_map/dot_general | solution.py:112
  104.4 4.3 %fusion.30 = f32[4096]{0:T(1024)S(1)} fusion(f32[512]{0:T(512)S(1)} %get-tuple-element.80, f32[512,4096]{1,0:T(8,128)} %copy-done.1), kind=kLoop, calls=%fused_computation.51 | loop fusion | flops 6287360 | bytes 8407040 | tf_op jit(solution)/shard_map/reduce_sum | solution.py:115
  108.7 59.9 %all-reduce = f32[4096]{0:T(1024)S(1)} all-reduce(f32[4096]{0:T(1024)S(1)} %fusion.30), channel_id=3, replica_groups=mesh['groups'=2,'frames'=16] {'frames'}, use_global_device_ids=true, to_apply=%region_15.16.clone | all-reduce | flops 4096 | bytes 32768
  168.7 12.4 %reduce-scatter.2.cloned.1.call-done = f32[256,256]{1,0:T(8,128)} async-done(((f32[4096,256]{1,0:T(8,128)}), f32[256,256]{1,0:T(8,128)}) %reduce-scatter.2.cloned.1.call-update) | async-done | bytes 262160 | tf_op jit(solution)/shard_map/reduce_scatter | solution.py:117
  181.1 1.8 broadcast_divide_fusion
  (113 shorter events, 15.1 us)
Async XLA Ops:
  7.2 49.5 %copy-start = (f32[256,768]{1,0:T(8,128)S(1)}, f32[256,768]{1,0:T(8,128)}, u32[]{:S(2)}) copy-start(f32[256,768]{1,0:T(8,128)} %param.18) | copy-start | bytes 2359300
  7.2 68.0 %all-gather.2.cloned.1.call-start = ((), (), s32[]{:S(2)}) async-start(), calls=%async_computation.1 | async-start | bytes 4456448 | tf_op jit(solution)/shard_map/all_gather | solution.py:107
  10.3 170.8 %reduce-scatter.2.cloned.1.call-start = ((), (), s32[]{:S(2)}) async-start(), calls=%async_computation.2 | async-start | bytes 4456448 | tf_op jit(solution)/shard_map/reduce_scatter | solution.py:117
  10.4 21.0 %copy-start.10 = (s32[2]{0:T(128)S(1)}, s32[2]{0:T(128)}, u32[]{:S(2)}) copy-start(s32[2]{0:T(128)} %param.13) | copy-start | bytes 28
  10.4 46.3 %copy-start.9 = (f32[256]{0:T(256)S(1)}, f32[256]{0:T(256)}, u32[]{:S(2)}) copy-start(f32[256]{0:T(256)} %param.17) | copy-start | bytes 3076
  10.4 5.7 %copy-start.2 = (f32[2,256,256]{2,1,0:T(8,128)S(1)}, f32[2,256,256]{2,1,0:T(8,128)}, u32[]{:S(2)}) copy-start(f32[2,256,256]{2,1,0:T(8,128)} %get-tuple-element.153) | copy-start | bytes 1572868 | tf_op jit(solution)/shard_map/while
  10.4 5.7 %copy-start.3 = (f32[256,256]{1,0:T(8,128)S(1)}, f32[256,256]{1,0:T(8,128)}, u32[]{:S(2)}) copy-start(f32[256,256]{1,0:T(8,128)} %get-tuple-element.156) | copy-start | bytes 786436 | tf_op jit(solution)/shard_map/while
  17.5 5.7 %copy-start.2 = (f32[2,256,256]{2,1,0:T(8,128)S(1)}, f32[2,256,256]{2,1,0:T(8,128)}, u32[]{:S(2)}) copy-start(f32[2,256,256]{2,1,0:T(8,128)} %get-tuple-element.153) | copy-start | bytes 1572868 | tf_op jit(solution)/shard_map/while
  17.5 5.7 %copy-start.3 = (f32[256,256]{1,0:T(8,128)S(1)}, f32[256,256]{1,0:T(8,128)}, u32[]{:S(2)}) copy-start(f32[256,256]{1,0:T(8,128)} %get-tuple-element.156) | copy-start | bytes 786436 | tf_op jit(solution)/shard_map/while
  25.6 6.0 %collective-permute-start = (f32[2,1,16,256]{3,2,0,1:T(8,128)S(1)}, f32[2,1,16,256]{3,2,0,1:T(8,128)S(1)}, u32[]{:S(2)}, u32[]{:S(2)}) collective-permute-start(f32[2,1,16,256]{3,2,0,1:T(8,128)S(1)} %get-tuple-element.75), channel_id=1, source_target_pairs={{0,1},{1,0},{2,3},{3,2},{4,5},{5,4},{6,7},{7,6},{8,9},{9,8},{10,11... | collective-permute-start | bytes 98312 | tf_op jit(solution)/shard_map/ppermute | solution.py:31
  26.1 8.2 %collective-permute-start.1 = (f32[2,1,16,256]{3,2,0,1:T(8,128)S(1)}, f32[2,1,16,256]{3,2,0,1:T(8,128)S(1)}, u32[]{:S(2)}, u32[]{:S(2)}) collective-permute-start(f32[2,1,16,256]{3,2,0,1:T(8,128)S(1)} %get-tuple-element.74), channel_id=1, source_target_pairs={{0,2},{1,3},{2,0},{3,1},{4,6},{5,7},{6,4},{7,5},{8,10},{9,11},{10,... | collective-permute-start | bytes 98312 | tf_op jit(solution)/shard_map/ppermute | solution.py:31
  28.7 5.7 %collective-permute-start.2 = (f32[2,1,16,256]{3,2,0,1:T(8,128)S(1)}, f32[2,1,16,256]{3,2,0,1:T(8,128)S(1)}, u32[]{:S(2)}, u32[]{:S(2)}) collective-permute-start(f32[2,1,16,256]{3,2,0,1:T(8,128)S(1)} %get-tuple-element.73), channel_id=1, source_target_pairs={{0,3},{1,2},{2,1},{3,0},{4,7},{5,6},{6,5},{7,4},{8,11},{9,10},{10,... | collective-permute-start | bytes 98312 | tf_op jit(solution)/shard_map/ppermute | solution.py:31
  28.8 8.3 %collective-permute-start.3 = (f32[2,1,16,256]{3,2,0,1:T(8,128)S(1)}, f32[2,1,16,256]{3,2,0,1:T(8,128)S(1)}, u32[]{:S(2)}, u32[]{:S(2)}) collective-permute-start(f32[2,1,16,256]{3,2,0,1:T(8,128)S(1)} %get-tuple-element.72), channel_id=1, source_target_pairs={{0,4},{1,5},{2,6},{3,7},{4,0},{5,1},{6,2},{7,3},{8,12},{9,13},{10,... | collective-permute-start | bytes 98312 | tf_op jit(solution)/shard_map/ppermute | solution.py:31
  30.6 6.5 %collective-permute-start.4 = (f32[2,1,16,256]{3,2,0,1:T(8,128)S(1)}, f32[2,1,16,256]{3,2,0,1:T(8,128)S(1)}, u32[]{:S(2)}, u32[]{:S(2)}) collective-permute-start(f32[2,1,16,256]{3,2,0,1:T(8,128)S(1)} %get-tuple-element.71), channel_id=1, source_target_pairs={{0,5},{1,4},{2,7},{3,6},{4,1},{5,0},{6,3},{7,2},{8,13},{9,12},{10,... | collective-permute-start | bytes 98312 | tf_op jit(solution)/shard_map/ppermute | solution.py:31
  31.5 9.1 %collective-permute-start.5 = (f32[2,1,16,256]{3,2,0,1:T(8,128)S(1)}, f32[2,1,16,256]{3,2,0,1:T(8,128)S(1)}, u32[]{:S(2)}, u32[]{:S(2)}) collective-permute-start(f32[2,1,16,256]{3,2,0,1:T(8,128)S(1)} %get-tuple-element.70), channel_id=1, source_target_pairs={{0,6},{1,7},{2,4},{3,5},{4,2},{5,3},{6,0},{7,1},{8,14},{9,15},{10,... | collective-permute-start | bytes 98312 | tf_op jit(solution)/shard_map/ppermute | solution.py:31
  34.3 6.5 %collective-permute-start.6 = (f32[2,1,16,256]{3,2,0,1:T(8,128)S(1)}, f32[2,1,16,256]{3,2,0,1:T(8,128)S(1)}, u32[]{:S(2)}, u32[]{:S(2)}) collective-permute-start(f32[2,1,16,256]{3,2,0,1:T(8,128)S(1)} %get-tuple-element.69), channel_id=1, source_target_pairs={{0,7},{1,6},{2,5},{3,4},{4,3},{5,2},{6,1},{7,0},{8,15},{9,14},{10,... | collective-permute-start | bytes 98312 | tf_op jit(solution)/shard_map/ppermute | solution.py:31
  34.4 9.9 %collective-permute-start.7 = (f32[2,1,16,256]{3,2,0,1:T(8,128)S(1)}, f32[2,1,16,256]{3,2,0,1:T(8,128)S(1)}, u32[]{:S(2)}, u32[]{:S(2)}) collective-permute-start(f32[2,1,16,256]{3,2,0,1:T(8,128)S(1)} %get-tuple-element.68), channel_id=1, source_target_pairs={{0,8},{1,9},{2,10},{3,11},{4,12},{5,13},{6,14},{7,15},{8,0},{9,1},... | collective-permute-start | bytes 98312 | tf_op jit(solution)/shard_map/ppermute | solution.py:31
  37.1 7.3 %collective-permute-start.8 = (f32[2,1,16,256]{3,2,0,1:T(8,128)S(1)}, f32[2,1,16,256]{3,2,0,1:T(8,128)S(1)}, u32[]{:S(2)}, u32[]{:S(2)}) collective-permute-start(f32[2,1,16,256]{3,2,0,1:T(8,128)S(1)} %get-tuple-element.67), channel_id=1, source_target_pairs={{0,9},{1,8},{2,11},{3,10},{4,13},{5,12},{6,15},{7,14},{8,1},{9,0},... | collective-permute-start | bytes 98312 | tf_op jit(solution)/shard_map/ppermute | solution.py:31
  37.1 11.6 %collective-permute-start.9 = (f32[2,1,16,256]{3,2,0,1:T(8,128)S(1)}, f32[2,1,16,256]{3,2,0,1:T(8,128)S(1)}, u32[]{:S(2)}, u32[]{:S(2)}) collective-permute-start(f32[2,1,16,256]{3,2,0,1:T(8,128)S(1)} %get-tuple-element.66), channel_id=1, source_target_pairs={{0,10},{1,11},{2,8},{3,9},{4,14},{5,15},{6,12},{7,13},{8,2},{9,3},... | collective-permute-start | bytes 98312 | tf_op jit(solution)/shard_map/ppermute | solution.py:31
  40.6 9.5 %collective-permute-start.10 = (f32[2,1,16,256]{3,2,0,1:T(8,128)S(1)}, f32[2,1,16,256]{3,2,0,1:T(8,128)S(1)}, u32[]{:S(2)}, u32[]{:S(2)}) collective-permute-start(f32[2,1,16,256]{3,2,0,1:T(8,128)S(1)} %get-tuple-element.65), channel_id=1, source_target_pairs={{0,11},{1,10},{2,9},{3,8},{4,15},{5,14},{6,13},{7,12},{8,3},{9,2},... | collective-permute-start | bytes 98312 | tf_op jit(solution)/shard_map/ppermute | solution.py:31
  40.7 9.4 %collective-permute-start.11 = (f32[2,1,16,256]{3,2,0,1:T(8,128)S(1)}, f32[2,1,16,256]{3,2,0,1:T(8,128)S(1)}, u32[]{:S(2)}, u32[]{:S(2)}) collective-permute-start(f32[2,1,16,256]{3,2,0,1:T(8,128)S(1)} %get-tuple-element.64), channel_id=1, source_target_pairs={{0,12},{1,13},{2,14},{3,15},{4,8},{5,9},{6,10},{7,11},{8,4},{9,5},... | collective-permute-start | bytes 98312 | tf_op jit(solution)/shard_map/ppermute | solution.py:31
  44.3 6.3 %collective-permute-start.12 = (f32[2,1,16,256]{3,2,0,1:T(8,128)S(1)}, f32[2,1,16,256]{3,2,0,1:T(8,128)S(1)}, u32[]{:S(2)}, u32[]{:S(2)}) collective-permute-start(f32[2,1,16,256]{3,2,0,1:T(8,128)S(1)} %get-tuple-element.63), channel_id=1, source_target_pairs={{0,13},{1,12},{2,15},{3,14},{4,9},{5,8},{6,11},{7,10},{8,5},{9,4},... | collective-permute-start | bytes 98312 | tf_op jit(solution)/shard_map/ppermute | solution.py:31
  44.3 8.7 %collective-permute-start.13 = (f32[2,1,16,256]{3,2,0,1:T(8,128)S(1)}, f32[2,1,16,256]{3,2,0,1:T(8,128)S(1)}, u32[]{:S(2)}, u32[]{:S(2)}) collective-permute-start(f32[2,1,16,256]{3,2,0,1:T(8,128)S(1)} %get-tuple-element.62), channel_id=1, source_target_pairs={{0,14},{1,15},{2,12},{3,13},{4,10},{5,11},{6,8},{7,9},{8,6},{9,7},... | collective-permute-start | bytes 98312 | tf_op jit(solution)/shard_map/ppermute | solution.py:31
  48.7 7.2 %collective-permute-start.14 = (f32[2,1,16,256]{3,2,0,1:T(8,128)S(1)}, f32[2,1,16,256]{3,2,0,1:T(8,128)S(1)}, u32[]{:S(2)}, u32[]{:S(2)}) collective-permute-start(f32[2,1,16,256]{3,2,0,1:T(8,128)S(1)} %get-tuple-element.61), channel_id=1, source_target_pairs={{0,15},{1,14},{2,13},{3,12},{4,11},{5,10},{6,9},{7,8},{8,7},{9,6},... | collective-permute-start | bytes 98312 | tf_op jit(solution)/shard_map/ppermute | solution.py:31
  63.7 6.0 %copy-start.6 = (f32[2,16,16,4,64]{4,3,2,1,0:T(4,128)S(1)}, f32[2,16,16,4,64]{4,3,2,1,0:T(4,128)}, u32[]{:S(2)}) copy-start(f32[2,16,16,4,64]{4,3,2,1,0:T(4,128)} %reshape.205) | copy-start | bytes 1572868
  74.9 28.3 %copy-start.5 = (f32[2,16,16,256]{3,2,1,0:T(8,128)}, f32[2,16,16,256]{3,2,1,0:T(8,128)S(1)}, u32[]{:S(2)}) copy-start(f32[2,16,16,256]{3,2,1,0:T(8,128)S(1)} %get-tuple-element.79) | copy-start | bytes 1572868
  84.9 3.2 %copy-start.1 = (f32[512,4096]{1,0:T(8,128)}, f32[512,4096]{1,0:T(8,128)S(1)}, u32[]{:S(2)}) copy-start(f32[512,4096]{1,0:T(8,128)S(1)} %get-tuple-element.81) | copy-start | bytes 25165828
  88.1 15.1 %copy-start.11 = (u32[32]{0:T(128)S(1)}, u32[32]{0:T(128)}, u32[]{:S(2)}) copy-start(u32[32]{0:T(128)} %constant.37) | copy-start | bytes 388
  103.1 65.5 %copy-start.7 = (f32[256]{0:T(256)S(1)}, f32[256]{0:T(256)}, u32[]{:S(2)}) copy-start(f32[256]{0:T(256)} %param.21) | copy-start | bytes 3076
  103.1 78.0 %copy-start.4 = (f32[256,256]{1,0:T(8,128)S(1)}, f32[256,256]{1,0:T(8,128)}, u32[]{:S(2)}) copy-start(f32[256,256]{1,0:T(8,128)} %param.20) | copy-start | bytes 786436
  168.7 14.2 %copy-start.8 = (f32[256]{0:T(256)}, f32[256]{0:T(256)S(1)}, u32[]{:S(2)}) copy-start(f32[256]{0:T(256)S(1)} %fusion.36) | copy-start | bytes 3076
Sparse Core Ops, SparseCore 0:
  10.7 58.7 all-gather.1
  103.3 77.7 reduce-scatter.1
